TPU v7x, 1024 devices: a whole 4x4x32 slice. The times are simulated.
1024 devices in a mesh: ctx: 64 (over z, x_lo), tp: 16 (over y, x_hi, core).
Axes of the slice: x: 4 (x_hi: 2, x_lo: 2; x = x_hi * 2 + x_lo), y: 4, z: 32, core: 2. Of those that a mesh axis runs over, the one named last changes fastest.
Arguments:
- queries: bfloat16 [16384, 8192], P('ctx', 'tp'), may hold values from -6 to 6
- keys: bfloat16 [16384, 2048], P('ctx', 'tp'), may hold values from -6 to 6
- values: bfloat16 [16384, 2048], P('ctx', 'tp'), may hold values from -6 to 6
- outputs: bfloat16 [16384, 8192], P('ctx', 'tp'), may hold values from -6 to 6
- out_grad: bfloat16 [16384, 8192], P('ctx', 'tp'), may hold values from -6 to 6
- log_norm: float32 [16384, 64], P('ctx', 'tp'), as said below
- block_mask: int32 [64, 4], P('ctx'), may hold values from 0 to 1, as said below
- counter_base: int32 [2], replicated, may hold values from 0 to 1048575
- q_weight: bfloat16 [4096, 8192], P(None, 'tp'), may hold values from -0.125 to 0.125
- k_weight: bfloat16 [4096, 2048], P(None, 'tp'), may hold values from -0.09375 to 0.09375
- v_weight: bfloat16 [4096, 2048], P(None, 'tp'), may hold values from -0.09375 to 0.09375
Outputs:
- input_grad: bfloat16 [16384, 4096], P('ctx', 'tp')
Inputs may be any that keep to these rules, and one draw needn't show every extreme that they name: block_mask[i, r] is 1 where query block i attends to key block i - r; column 0 and the row of the last block are all 1. log_norm lies between log(512) - 0.5 and log(512) + 2.5.
All inputs are finite; a program needn't handle non-finite values.
Results may differ from a plain program's by a relative error of at most 0.015.
Values may be sent and summed in bfloat16 or wider, within the bound.
A program may use at most 32 MiB of HBM per device.

v0:
```python
import jax
import jax.numpy as jnp
from jax import lax
from jax.sharding import PartitionSpec as P

keep_level = 103
keep_scale = 1024.0 / 921.0


def shifted(array, axis, by):
    devices = lax.axis_size(axis)
    pairs = [(i, i + by) for i in range(devices) if 0 <= i + by < devices]
    return lax.ppermute(array, axis, pairs)


def passed_along(value, axis, steps):
    count = lax.axis_size(axis)
    pairs = [(source, (source + steps) % count) for source in range(count)]
    return lax.ppermute(value, axis, pairs)


def keep_mask(head_ids, query_pos, key_pos, seed_value):
    mixed = (
        head_ids[:, None, None] * 83492791
        + query_pos[None, :, None] * 73856093
        + key_pos[None, None, :] * 19349663
        + seed_value
    )
    mixed = mixed ^ lax.shift_right_logical(mixed, jnp.int32(15))
    mixed = mixed * 739982445
    mixed = mixed ^ lax.shift_right_logical(mixed, jnp.int32(12))
    mixed = mixed * 695872825
    mixed = mixed ^ lax.shift_right_logical(mixed, jnp.int32(15))
    return mixed & 1023 >= keep_level


def pair_grads(
    query_blk,
    grad_out,
    norm_blk,
    row_delta,
    key_blk,
    value_blk,
    query_start,
    key_start,
    active,
    head_ids,
    counter_base,
    window,
):
    rows_count = query_blk.shape[0]
    scaling = query_blk.shape[2] ** (-0.5)
    scores = (
        jnp.einsum("qhd,kd->hqk", query_blk, key_blk, preferred_element_type=jnp.float32) * scaling
    )
    query_pos = query_start + jnp.arange(rows_count, dtype=jnp.int32)
    key_pos = key_start + jnp.arange(rows_count, dtype=jnp.int32)
    spacing = query_pos[:, None] - key_pos[None, :]
    allowed = (spacing >= 0) & (spacing < window) & active
    probs = jnp.where(
        allowed[None], jnp.exp(scores - jnp.transpose(norm_blk)[:, :, None]), jnp.float32(0.0)
    )
    kept = keep_mask(
        head_ids, query_pos + counter_base[1], key_pos + counter_base[1], counter_base[0]
    )
    dropped = jnp.where(kept, probs * keep_scale, jnp.float32(0.0)).astype(jnp.bfloat16)
    grad_value = jnp.einsum("hqk,qhd->kd", dropped, grad_out, preferred_element_type=jnp.float32)
    grad_probs = jnp.einsum("qhd,kd->hqk", grad_out, value_blk, preferred_element_type=jnp.float32)
    grad_scores = (
        probs
        * (
            jnp.where(kept, grad_probs * keep_scale, jnp.float32(0.0))
            - jnp.transpose(row_delta)[:, :, None]
        )
    ).astype(jnp.bfloat16)
    grad_query = (
        jnp.einsum("hqk,kd->qhd", grad_scores, key_blk, preferred_element_type=jnp.float32)
        * scaling
    )
    grad_key = (
        jnp.einsum("hqk,qhd->kd", grad_scores, query_blk, preferred_element_type=jnp.float32)
        * scaling
    )
    return (grad_query, grad_key, grad_value)


def on_device(
    queries,
    keys,
    values,
    outputs,
    out_grad,
    log_norm,
    block_mask,
    counter_base,
    q_weight,
    k_weight,
    v_weight,
):
    rows_count = queries.shape[0]
    head_count = log_norm.shape[1]
    head_dim = keys.shape[1]
    window = 3 * rows_count + rows_count // 2
    block_id = lax.axis_index("ctx")
    group_id = lax.axis_index("tp")
    head_ids = group_id * head_count + jnp.arange(head_count, dtype=jnp.int32)
    query_blk = queries.reshape(rows_count, head_count, head_dim)
    grad_out = out_grad.reshape(rows_count, head_count, head_dim)
    row_delta = jnp.sum(
        grad_out.astype(jnp.float32)
        * outputs.reshape(rows_count, head_count, head_dim).astype(jnp.float32),
        axis=2,
    )
    mask_row = block_mask[0]
    key_blk = keys
    value_blk = values
    grad_query = jnp.zeros((rows_count, head_count, head_dim), jnp.float32)
    empty_grad = jnp.zeros((rows_count, head_dim), jnp.float32)
    carried = (empty_grad, empty_grad)
    for offset in range(block_mask.shape[1]):
        if offset > 0:
            key_blk, value_blk = shifted((key_blk, value_blk), "ctx", 1)
        source = block_id - offset
        active = (source >= 0) & (mask_row[offset] == 1)
        add_query, add_key, add_value = pair_grads(
            query_blk,
            grad_out,
            log_norm,
            row_delta,
            key_blk,
            value_blk,
            block_id * rows_count,
            source * rows_count,
            active,
            head_ids,
            counter_base,
            window,
        )
        grad_query = grad_query + add_query
        if offset > 0:
            carried = (
                passed_along(carried[0].astype(jnp.bfloat16), "ctx", 1).astype(jnp.float32),
                passed_along(carried[1].astype(jnp.bfloat16), "ctx", 1).astype(jnp.float32),
            )
        carried = (carried[0] + add_key, carried[1] + add_value)
    steps_back = 1 - block_mask.shape[1]
    grad_key, grad_value = (
        passed_along(carried[0].astype(jnp.bfloat16), "ctx", steps_back).astype(jnp.float32),
        passed_along(carried[1].astype(jnp.bfloat16), "ctx", steps_back).astype(jnp.float32),
    )
    contract = (((1,), (1,)), ((), ()))
    query_round = grad_query.reshape(rows_count, head_count * head_dim).astype(jnp.bfloat16)
    partial_term = lax.dot_general(
        query_round, q_weight, contract, preferred_element_type=jnp.float32
    )
    partial_term = partial_term + lax.dot_general(
        grad_key.astype(jnp.bfloat16), k_weight, contract, preferred_element_type=jnp.float32
    )
    partial_term = partial_term + lax.dot_general(
        grad_value.astype(jnp.bfloat16), v_weight, contract, preferred_element_type=jnp.float32
    )
    return lax.psum_scatter(
        partial_term.astype(jnp.bfloat16), "tp", scatter_dimension=1, tiled=True
    )


def solution(mesh):
    return jax.shard_map(
        on_device,
        mesh=mesh,
        in_specs=(
            P("ctx", "tp"),
            P("ctx", "tp"),
            P("ctx", "tp"),
            P("ctx", "tp"),
            P("ctx", "tp"),
            P("ctx", "tp"),
            P("ctx", None),
            P(),
            P(None, "tp"),
            P(None, "tp"),
            P(None, "tp"),
        ),
        out_specs=P("ctx", "tp"),
        check_vma=False,
    )
```

profile of v0, /device:TPU:1, one launch (start us, length us, event | category | flops | bytes accessed | tf_op | source)
XLA Modules:
  0.0 232.0 jit_solution(16032162103115718873)
XLA Ops:
  6.5 4.1 %collective-permute-start.1 = (bf16[256,128]{1,0:T(8,128)(2,1)}, bf16[256,128]{1,0:T(8,128)(2,1)S(1)}, u32[]{:S(2)}, u32[]{:S(2)}) collective-permute-start(bf16[256,128]{1,0:T(8,128)(2,1)} %param.13), channel_id=1, source_target_pairs={{0,16},{16,32},{32,48},{48,64},{64,80},{80,96},{96,112},{112,128},... | collective-permute-start | bytes 196616 | tf_op jit(solution)/shard_map/ppermute | solution.py:13
  10.6 3.5 %collective-permute-start = (bf16[256,128]{1,0:T(8,128)(2,1)}, bf16[256,128]{1,0:T(8,128)(2,1)S(1)}, u32[]{:S(2)}, u32[]{:S(2)}) collective-permute-start(bf16[256,128]{1,0:T(8,128)(2,1)} %param.12), channel_id=1, source_target_pairs={{0,16},{16,32},{32,48},{48,64},{64,80},{80,96},{96,112},{112,128},... | collective-permute-start | bytes 196616 | tf_op jit(solution)/shard_map/ppermute | solution.py:13
  14.2 1.3 fusion.163
  15.5 0.6 add_multiply_fusion.4
  16.1 0.7 iota_add_fusion.3
  16.8 1.5 fusion.162
  21.0 1.0 reshape.247
  22.0 1.2 reshape.248
  23.2 0.4 multiply_reduce_fusion
  23.7 0.4 fusion.96
  24.1 1.3 fusion.32
  25.4 1.3 fusion.33
  26.8 0.3 fusion.43
  27.1 3.1 %collective-permute-start.6 = (bf16[256,128]{1,0:T(8,128)(2,1)S(1)}, bf16[256,128]{1,0:T(8,128)(2,1)S(1)}, u32[]{:S(2)}, u32[]{:S(2)}) collective-permute-start(bf16[256,128]{1,0:T(8,128)(2,1)S(1)} %fusion.43), channel_id=1, source_target_pairs={{0,16},{16,32},{32,48},{48,64},{64,80},{80,96},{96,112},{112,128},... | collective-permute-start | bytes 196616 | tf_op jit(solution)/shard_map/ppermute | solution.py:19
  30.2 1.3 fusion.44
  31.5 3.5 %collective-permute-start.10 = (bf16[256,128]{1,0:T(8,128)(2,1)S(1)}, bf16[256,128]{1,0:T(8,128)(2,1)S(1)}, u32[]{:S(2)}, u32[]{:S(2)}) collective-permute-start(bf16[256,128]{1,0:T(8,128)(2,1)S(1)} %fusion.44), channel_id=1, source_target_pairs={{0,16},{16,32},{32,48},{48,64},{64,80},{80,96},{96,112},{112,128},... | collective-permute-start | bytes 196616 | tf_op jit(solution)/shard_map/ppermute | solution.py:19
  35.0 0.7 add_multiply_fusion.2
  35.7 0.7 add_multiply_fusion.1
  36.6 0.7 add_multiply_fusion
  37.3 0.4 fusion.24
  37.7 1.3 fusion.34
  39.0 5.0 %collective-permute-done.6 = bf16[256,128]{1,0:T(8,128)(2,1)S(1)} collective-permute-done((bf16[256,128]{1,0:T(8,128)(2,1)S(1)}, bf16[256,128]{1,0:T(8,128)(2,1)S(1)}, u32[]{:S(2)}, u32[]{:S(2)}) %collective-permute-start.6) | collective-permute-done | bytes 65568 | tf_op jit(solution)/shard_map/ppermute | solution.py:19
  44.0 0.3 add_convert_fusion.5
  44.3 1.9 collective-permute-start.7
  46.2 1.0 collective-permute-done.10
  47.2 1.3 add_convert_fusion.2
  48.5 1.9 collective-permute-start.11
  50.4 1.3 collective-permute-start.3
  51.7 3.4 %collective-permute-start.2 = (bf16[256,128]{1,0:T(8,128)(2,1)S(1)}, bf16[256,128]{1,0:T(8,128)(2,1)S(1)}, u32[]{:S(2)}, u32[]{:S(2)}) collective-permute-start(bf16[256,128]{1,0:T(8,128)(2,1)S(1)} %collective-permute-done), channel_id=1, source_target_pairs={{0,16},{16,32},{32,48},{48,64},{64,80},{80,96},{96,112},{112,128},... | collective-permute-start | bytes 196616 | tf_op jit(solution)/shard_map/ppermute | solution.py:13
  55.4 1.0 collective-permute-done.2
  56.4 0.4 fusion.16
  56.8 1.3 convolution_bitcast_fusion.1
  58.1 1.3 fusion.35
  59.7 3.7 %collective-permute-start.8 = (bf16[256,128]{1,0:T(8,128)(2,1)S(1)}, bf16[256,128]{1,0:T(8,128)(2,1)S(1)}, u32[]{:S(2)}, u32[]{:S(2)}) collective-permute-start(bf16[256,128]{1,0:T(8,128)(2,1)S(1)} %add_convert_fusion.4), channel_id=1, source_target_pairs={{0,16},{16,32},{32,48},{48,64},{64,80},{80,96},{96,112},{112,128},... | collective-permute-start | bytes 196616 | tf_op jit(solution)/shard_map/ppermute | solution.py:19
  63.4 4.4 %collective-permute-start.12 = (bf16[256,128]{1,0:T(8,128)(2,1)S(1)}, bf16[256,128]{1,0:T(8,128)(2,1)S(1)}, u32[]{:S(2)}, u32[]{:S(2)}) collective-permute-start(bf16[256,128]{1,0:T(8,128)(2,1)S(1)} %add_convert_fusion.1), channel_id=1, source_target_pairs={{0,16},{16,32},{32,48},{48,64},{64,80},{80,96},{96,112},{112,128},... | collective-permute-start | bytes 196616 | tf_op jit(solution)/shard_map/ppermute | solution.py:19
  67.9 2.2 collective-permute-start.5
  70.1 4.4 %collective-permute-start.4 = (bf16[256,128]{1,0:T(8,128)(2,1)S(1)}, bf16[256,128]{1,0:T(8,128)(2,1)S(1)}, u32[]{:S(2)}, u32[]{:S(2)}) collective-permute-start(bf16[256,128]{1,0:T(8,128)(2,1)S(1)} %collective-permute-done.2), channel_id=1, source_target_pairs={{0,16},{16,32},{32,48},{48,64},{64,80},{80,96},{96,112},{112,128},... | collective-permute-start | bytes 196616 | tf_op jit(solution)/shard_map/ppermute | solution.py:13
  74.8 1.2 collective-permute-done.4
  76.0 0.4 fusion.8
  76.4 1.3 convolution_bitcast_fusion
  77.7 1.5 fusion.36
  79.4 8.4 %collective-permute-start.9 = (bf16[256,128]{1,0:T(8,128)(2,1)S(1)}, bf16[256,128]{1,0:T(8,128)(2,1)S(1)}, u32[]{:S(2)}, u32[]{:S(2)}) collective-permute-start(bf16[256,128]{1,0:T(8,128)(2,1)S(1)} %add_convert_fusion.3), channel_id=1, source_target_pairs={{0,976},{16,992},{32,1008},{48,0},{64,16},{80,32},{96,48},{112,64}... | collective-permute-start | bytes 196616 | tf_op jit(solution)/shard_map/ppermute | solution.py:19
  87.9 5.8 %collective-permute-start.13 = (bf16[256,128]{1,0:T(8,128)(2,1)S(1)}, bf16[256,128]{1,0:T(8,128)(2,1)S(1)}, u32[]{:S(2)}, u32[]{:S(2)}) collective-permute-start(bf16[256,128]{1,0:T(8,128)(2,1)S(1)} %add_convert_fusion), channel_id=1, source_target_pairs={{0,976},{16,992},{32,1008},{48,0},{64,16},{80,32},{96,48},{112,64}... | collective-permute-start | bytes 196616 | tf_op jit(solution)/shard_map/ppermute | solution.py:19
  94.0 1.3 fusion.164
  95.4 0.7 convolution_add_fusion.1
  96.1 0.5 copy-done.2
  96.6 2.0 fusion
  98.6 126.5 %reduce-scatter.2.cloned.1.call-done = bf16[256,256]{1,0:T(8,128)(2,1)} async-done(((bf16[256,4096]{1,0:T(8,128)(2,1)}), bf16[256,256]{1,0:T(8,128)(2,1)}) %reduce-scatter.2.cloned.1.call-update) | async-done | bytes 131088 | tf_op jit(solution)/shard_map/reduce_scatter | solution.py:162
  (42 shorter events, 2.0 us)
Async XLA Ops:
  6.5 88.8 %copy-start = (bf16[4096,128]{1,0:T(8,128)(2,1)S(1)}, bf16[4096,128]{1,0:T(8,128)(2,1)}, u32[]{:S(2)}) copy-start(bf16[4096,128]{1,0:T(8,128)(2,1)} %param.20) | copy-start | bytes 3145732
  6.5 18.9 %copy-start.6 = (bf16[256,128]{1,0:T(8,128)(2,1)S(1)}, bf16[256,128]{1,0:T(8,128)(2,1)}, u32[]{:S(2)}) copy-start(bf16[256,128]{1,0:T(8,128)(2,1)} %param.13) | copy-start | bytes 196612
  6.5 18.9 %copy-start.4 = (bf16[256,512]{1,0:T(8,128)(2,1)S(1)}, bf16[256,512]{1,0:T(8,128)(2,1)}, u32[]{:S(2)}) copy-start(bf16[256,512]{1,0:T(8,128)(2,1)} %param.15) | copy-start | bytes 786436
  6.5 218.6 %reduce-scatter.2.cloned.1.call-start = ((), (), s32[]{:S(2)}) async-start(), calls=%async_computation.1 | async-start | bytes 2228224 | tf_op jit(solution)/shard_map/reduce_scatter | solution.py:162
  6.5 31.1 %collective-permute-start.1 = (bf16[256,128]{1,0:T(8,128)(2,1)}, bf16[256,128]{1,0:T(8,128)(2,1)S(1)}, u32[]{:S(2)}, u32[]{:S(2)}) collective-permute-start(bf16[256,128]{1,0:T(8,128)(2,1)} %param.13), channel_id=1, source_target_pairs={{0,16},{16,32},{32,48},{48,64},{64,80},{80,96},{96,112},{112,128},... | collective-permute-start | bytes 196616 | tf_op jit(solution)/shard_map/ppermute | solution.py:13
  10.6 26.6 %collective-permute-start = (bf16[256,128]{1,0:T(8,128)(2,1)}, bf16[256,128]{1,0:T(8,128)(2,1)S(1)}, u32[]{:S(2)}, u32[]{:S(2)}) collective-permute-start(bf16[256,128]{1,0:T(8,128)(2,1)} %param.12), channel_id=1, source_target_pairs={{0,16},{16,32},{32,48},{48,64},{64,80},{80,96},{96,112},{112,128},... | collective-permute-start | bytes 196616 | tf_op jit(solution)/shard_map/ppermute | solution.py:13
  22.0 4.8 %copy-start.3 = (bf16[256,512]{1,0:T(8,128)(2,1)S(1)}, bf16[256,512]{1,0:T(8,128)(2,1)}, u32[]{:S(2)}) copy-start(bf16[256,512]{1,0:T(8,128)(2,1)} %param.11) | copy-start | bytes 786436
  25.4 10.9 %copy-start.5 = (bf16[256,128]{1,0:T(8,128)(2,1)S(1)}, bf16[256,128]{1,0:T(8,128)(2,1)}, u32[]{:S(2)}) copy-start(bf16[256,128]{1,0:T(8,128)(2,1)} %param.12) | copy-start | bytes 196612
  26.8 10.5 %copy-start.7 = (f32[256,4]{0,1:T(4,128)S(1)}, f32[256,4]{0,1:T(4,128)}, u32[]{:S(2)}) copy-start(f32[256,4]{0,1:T(4,128)} %param.16) | copy-start | bytes 12292
  27.1 16.9 %collective-permute-start.6 = (bf16[256,128]{1,0:T(8,128)(2,1)S(1)}, bf16[256,128]{1,0:T(8,128)(2,1)S(1)}, u32[]{:S(2)}, u32[]{:S(2)}) collective-permute-start(bf16[256,128]{1,0:T(8,128)(2,1)S(1)} %fusion.43), channel_id=1, source_target_pairs={{0,16},{16,32},{32,48},{48,64},{64,80},{80,96},{96,112},{112,128},... | collective-permute-start | bytes 196616 | tf_op jit(solution)/shard_map/ppermute | solution.py:19
  31.5 15.7 %collective-permute-start.10 = (bf16[256,128]{1,0:T(8,128)(2,1)S(1)}, bf16[256,128]{1,0:T(8,128)(2,1)S(1)}, u32[]{:S(2)}, u32[]{:S(2)}) collective-permute-start(bf16[256,128]{1,0:T(8,128)(2,1)S(1)} %fusion.44), channel_id=1, source_target_pairs={{0,16},{16,32},{32,48},{48,64},{64,80},{80,96},{96,112},{112,128},... | collective-permute-start | bytes 196616 | tf_op jit(solution)/shard_map/ppermute | solution.py:19
  44.3 15.4 %collective-permute-start.7 = (bf16[256,128]{1,0:T(8,128)(2,1)S(1)}, bf16[256,128]{1,0:T(8,128)(2,1)S(1)}, u32[]{:S(2)}, u32[]{:S(2)}) collective-permute-start(bf16[256,128]{1,0:T(8,128)(2,1)S(1)} %add_convert_fusion.5), channel_id=1, source_target_pairs={{0,16},{16,32},{32,48},{48,64},{64,80},{80,96},{96,112},{112,128},... | collective-permute-start | bytes 196616 | tf_op jit(solution)/shard_map/ppermute | solution.py:19
  48.5 15.0 %collective-permute-start.11 = (bf16[256,128]{1,0:T(8,128)(2,1)S(1)}, bf16[256,128]{1,0:T(8,128)(2,1)S(1)}, u32[]{:S(2)}, u32[]{:S(2)}) collective-permute-start(bf16[256,128]{1,0:T(8,128)(2,1)S(1)} %add_convert_fusion.2), channel_id=1, source_target_pairs={{0,16},{16,32},{32,48},{48,64},{64,80},{80,96},{96,112},{112,128},... | collective-permute-start | bytes 196616 | tf_op jit(solution)/shard_map/ppermute | solution.py:19
  50.4 7.7 %collective-permute-start.3 = (bf16[256,128]{1,0:T(8,128)(2,1)S(1)}, bf16[256,128]{1,0:T(8,128)(2,1)S(1)}, u32[]{:S(2)}, u32[]{:S(2)}) collective-permute-start(bf16[256,128]{1,0:T(8,128)(2,1)S(1)} %collective-permute-done.1), channel_id=1, source_target_pairs={{0,16},{16,32},{32,48},{48,64},{64,80},{80,96},{96,112},{112,128},... | collective-permute-start | bytes 196616 | tf_op jit(solution)/shard_map/ppermute | solution.py:13
  51.7 4.7 %collective-permute-start.2 = (bf16[256,128]{1,0:T(8,128)(2,1)S(1)}, bf16[256,128]{1,0:T(8,128)(2,1)S(1)}, u32[]{:S(2)}, u32[]{:S(2)}) collective-permute-start(bf16[256,128]{1,0:T(8,128)(2,1)S(1)} %collective-permute-done), channel_id=1, source_target_pairs={{0,16},{16,32},{32,48},{48,64},{64,80},{80,96},{96,112},{112,128},... | collective-permute-start | bytes 196616 | tf_op jit(solution)/shard_map/ppermute | solution.py:13
  59.7 19.7 %collective-permute-start.8 = (bf16[256,128]{1,0:T(8,128)(2,1)S(1)}, bf16[256,128]{1,0:T(8,128)(2,1)S(1)}, u32[]{:S(2)}, u32[]{:S(2)}) collective-permute-start(bf16[256,128]{1,0:T(8,128)(2,1)S(1)} %add_convert_fusion.4), channel_id=1, source_target_pairs={{0,16},{16,32},{32,48},{48,64},{64,80},{80,96},{96,112},{112,128},... | collective-permute-start | bytes 196616 | tf_op jit(solution)/shard_map/ppermute | solution.py:19
  63.4 24.4 %collective-permute-start.12 = (bf16[256,128]{1,0:T(8,128)(2,1)S(1)}, bf16[256,128]{1,0:T(8,128)(2,1)S(1)}, u32[]{:S(2)}, u32[]{:S(2)}) collective-permute-start(bf16[256,128]{1,0:T(8,128)(2,1)S(1)} %add_convert_fusion.1), channel_id=1, source_target_pairs={{0,16},{16,32},{32,48},{48,64},{64,80},{80,96},{96,112},{112,128},... | collective-permute-start | bytes 196616 | tf_op jit(solution)/shard_map/ppermute | solution.py:19
  67.9 9.8 %collective-permute-start.5 = (bf16[256,128]{1,0:T(8,128)(2,1)S(1)}, bf16[256,128]{1,0:T(8,128)(2,1)S(1)}, u32[]{:S(2)}, u32[]{:S(2)}) collective-permute-start(bf16[256,128]{1,0:T(8,128)(2,1)S(1)} %collective-permute-done.3), channel_id=1, source_target_pairs={{0,16},{16,32},{32,48},{48,64},{64,80},{80,96},{96,112},{112,128},... | collective-permute-start | bytes 196616 | tf_op jit(solution)/shard_map/ppermute | solution.py:13
  70.1 5.9 %collective-permute-start.4 = (bf16[256,128]{1,0:T(8,128)(2,1)S(1)}, bf16[256,128]{1,0:T(8,128)(2,1)S(1)}, u32[]{:S(2)}, u32[]{:S(2)}) collective-permute-start(bf16[256,128]{1,0:T(8,128)(2,1)S(1)} %collective-permute-done.2), channel_id=1, source_target_pairs={{0,16},{16,32},{32,48},{48,64},{64,80},{80,96},{96,112},{112,128},... | collective-permute-start | bytes 196616 | tf_op jit(solution)/shard_map/ppermute | solution.py:13
  77.6 16.4 %copy-start.1 = (bf16[4096,512]{1,0:T(8,128)(2,1)S(1)}, bf16[4096,512]{1,0:T(8,128)(2,1)}, u32[]{:S(2)}) copy-start(bf16[4096,512]{1,0:T(8,128)(2,1)} %param.19) | copy-start | bytes 12582916
  79.4 15.9 %collective-permute-start.9 = (bf16[256,128]{1,0:T(8,128)(2,1)S(1)}, bf16[256,128]{1,0:T(8,128)(2,1)S(1)}, u32[]{:S(2)}, u32[]{:S(2)}) collective-permute-start(bf16[256,128]{1,0:T(8,128)(2,1)S(1)} %add_convert_fusion.3), channel_id=1, source_target_pairs={{0,976},{16,992},{32,1008},{48,0},{64,16},{80,32},{96,48},{112,64}... | collective-permute-start | bytes 196616 | tf_op jit(solution)/shard_map/ppermute | solution.py:19
  87.9 8.2 %collective-permute-start.13 = (bf16[256,128]{1,0:T(8,128)(2,1)S(1)}, bf16[256,128]{1,0:T(8,128)(2,1)S(1)}, u32[]{:S(2)}, u32[]{:S(2)}) collective-permute-start(bf16[256,128]{1,0:T(8,128)(2,1)S(1)} %add_convert_fusion), channel_id=1, source_target_pairs={{0,976},{16,992},{32,1008},{48,0},{64,16},{80,32},{96,48},{112,64}... | collective-permute-start | bytes 196616 | tf_op jit(solution)/shard_map/ppermute | solution.py:19
  95.3 1.2 copy-start.2
Sparse Core Ops, SparseCore 0:
  98.8 126.3 reduce-scatter.1
where the time goes:
time: 234 us; the launch traced here: 232 us
  waiting for transfers between devices  135 us (58%)
  starting transfers between devices  51.7 us (22%)
  matrix products  19.2 us (8%)
  between operations  16.7 us (7%)
  local copies, waits for them, and re-layouts  5.55 us (2%)
  other arithmetic  4.11 us (2%)
    reduce_scatter x1, waiting for transfers between devices, on_device(): lax.psum_scatter(partial_term.astype(jnp.bfloat16), 'tp', scatter_dimensi...  127 us
    ppermute x8, starting transfers between devices, passed_along(): return lax.ppermute(value, axis, pairs)  32.8 us
    ppermute x6, starting transfers between devices, shifted(): return lax.ppermute(array, axis, pairs)  18.9 us
    ppermute x8, waiting for transfers between devices, passed_along(): return lax.ppermute(value, axis, pairs)  6 us
    dot_general x4, matrix products, pair_grads(): jnp.einsum('qhd,kd->hqk', grad_out, value_blk, preferred_element_type=jnp...  5.41 us
    dot_general x4, matrix products, pair_grads(): jnp.einsum('hqk,qhd->kd', dropped, grad_out, preferred_element_type=jnp.f...  5.05 us
  transfers between devices with their start and end apart: 15, of which 5 were waited for; matrix products, arithmetic and copies ran while one was open for 11% of the time, Pallas kernels for 0%

commit v1 on v0

v1 whole, which is shorter than its diff:
```python
import functools

import jax
import jax.numpy as jnp
from jax import lax
from jax.experimental import pallas as pl
from jax.experimental.pallas import tpu as pltpu
from jax.sharding import PartitionSpec as P

MESH = pl.DeviceIdType.MESH
keep_level = 103
keep_scale = 1024.0 / 921.0
ROWS = 16
NT = (((1,), (1,)), ((), ()))
NN = (((1,), (0,)), ((), ()))
TN = (((0,), (0,)), ((), ()))
HOPS = ((2, 1), (2, 0), (1, 1), (3, 1), (0, 1), (1, 0), (3, 0), (0, 0))
OFFSETS = (2, 1, 3, 0)


def dot(a, b, dims):
    return lax.dot_general(a, b, dims, preferred_element_type=jnp.float32)


def kernel(
    q_hbm,
    k_hbm,
    v_hbm,
    o_hbm,
    g_hbm,
    norm_hbm,
    mask_smem,
    base_smem,
    wq_hbm,
    wk_hbm,
    wv_hbm,
    out_ref,
    q_st,
    g_st,
    o_st,
    norm_in,
    own_kv,
    got_kv,
    kept,
    s_buf,
    dp_buf,
    pk_buf,
    ds_buf,
    rows_buf,
    dq_acc,
    own_acc,
    back_out,
    back_in,
    grads,
    kv_grads,
    wq,
    wkv,
    terms,
    pair_out,
    pair_in,
    far_out,
    far_in,
    load_sem,
    kv_send,
    kv_recv,
    back_send,
    back_recv,
    pair_send,
    pair_recv,
    far_send,
    far_recv,
):
    tok = k_hbm.shape[0]
    hd = k_hbm.shape[1]
    heads = q_hbm.shape[1] // hd
    wide = heads * tok
    blocks = lax.axis_size("ctx")
    block_id = lax.axis_index("ctx")
    group_id = lax.axis_index("tp")
    y_pos = group_id // 4
    x_pos = (group_id // 2) % 2
    core = group_id % 2
    scaling = hd ** (-0.5)

    def ctx_at(steps):
        return lax.rem(block_id + steps + blocks, blocks)

    def chip_at(hop):
        return lax.rem(y_pos + hop[0], 4) * 2 + lax.rem(x_pos + hop[1], 2)

    partner = group_id + 1 - 2 * core

    loads = []

    def load(src, dst):
        copy = pltpu.make_async_copy(src, dst, load_sem.at[len(loads)])
        copy.start()
        loads.append(copy)
        return copy

    kv_loads = [load(k_hbm, own_kv.at[0]), load(v_hbm, own_kv.at[1])]
    head_loads = []
    for src, dst in ((g_hbm, g_st), (o_hbm, o_st), (q_hbm, q_st)):
        for h in range(heads):
            head_loads.append(
                load(src.at[:, pl.ds(h * hd, hd)], dst.at[pl.ds(h * tok, tok), :])
            )
    norm_load = load(norm_hbm, norm_in)
    weight_loads = [
        load(wq_hbm, wq),
        load(wk_hbm, wkv.at[:, pl.ds(0, hd)]),
        load(wv_hbm, wkv.at[:, pl.ds(hd, hd)]),
    ]

    barrier = pltpu.get_barrier_semaphore()
    peers = [(ctx_at(r), group_id) for r in (1, -1, 2, -2, 3, -3)]
    peers.append((block_id, partner))
    peers += [(block_id, chip_at(hop) * 2 + core) for hop in HOPS[:-1]]
    for peer in peers:
        pl.semaphore_signal(barrier, inc=1, device_id=peer, device_id_type=MESH)
    pl.semaphore_wait(barrier, len(peers))

    for copy in kv_loads:
        copy.wait()
    kv_copies = {}
    for r in (1, 2, 3):
        for part in range(2):
            copy = pltpu.make_async_remote_copy(
                src_ref=own_kv.at[part],
                dst_ref=got_kv.at[r - 1, part],
                send_sem=kv_send.at[r - 1, part],
                recv_sem=kv_recv.at[r - 1, part],
                device_id=(ctx_at(r), group_id),
                device_id_type=MESH,
            )
            kv_copies[r, part] = copy
    for r in (2, 1, 3):
        for part in range(2):
            kv_copies[r, part].start()

    lane = lax.broadcasted_iota(jnp.int32, (ROWS, wide), 1)
    sub = lax.broadcasted_iota(jnp.int32, (ROWS, wide), 0)
    head = lane // tok
    query = lane - head * tok
    spread = query - sub
    seed = base_smem[0]
    shift = base_smem[1]
    mixed_base = (
        (head + group_id * heads) * 83492791
        + query * 73856093
        + sub * 19349663
        + ((block_id * tok + shift) * 73856093 + seed)
    )

    def mask_rows(r):
        def step(i, carry):
            key_start = (block_id - r) * tok + i * ROWS + shift
            mixed = mixed_base + key_start * 19349663
            mixed = mixed ^ lax.shift_right_logical(mixed, jnp.int32(15))
            mixed = mixed * 739982445
            mixed = mixed ^ lax.shift_right_logical(mixed, jnp.int32(12))
            mixed = mixed * 695872825
            mixed = mixed ^ lax.shift_right_logical(mixed, jnp.int32(15))
            kept[r, pl.ds(pl.multiple_of(i * ROWS, ROWS), ROWS), :] = jnp.where(
                mixed & 1023 >= keep_level, jnp.float32(1.0), jnp.float32(0.0)
            )
            return carry

        lax.fori_loop(0, tok // ROWS, step, 0)

    for r in OFFSETS:
        mask_rows(r)

    for copy in head_loads:
        copy.wait()
    norm_load.wait()
    for h in range(heads):
        rows = pl.ds(h * tok, tok)
        prod = g_st[rows, :].astype(jnp.float32) * o_st[rows, :].astype(jnp.float32)
        delta = jnp.sum(jnp.transpose(prod), axis=0, keepdims=True)
        rows_buf[0:1, rows] = delta * jnp.float32(1.0 / keep_scale)
        column = jnp.broadcast_to(norm_in[:, h : h + 1], (tok, hd))
        norm_row = jnp.transpose(column)[0:1, :]
        for r in range(4):
            active = (block_id - r >= 0) & (mask_smem[0, r] == 1)
            push = jnp.where(active, jnp.float32(0.0), jnp.float32(1e30))
            rows_buf[r + 1 : r + 2, rows] = norm_row + push

    back_copies = {}
    for place, r in enumerate(OFFSETS):
        if r > 0:
            for part in range(2):
                kv_copies[r, part].wait_recv()
            key_blk = got_kv.at[r - 1, 0]
            value_blk = got_kv.at[r - 1, 1]
        else:
            key_blk = own_kv.at[0]
            value_blk = own_kv.at[1]
        s_buf[...] = dot(key_blk[...], q_st[...], NT)
        dp_buf[...] = dot(value_blk[...], g_st[...], NT)

        def pair_rows(i, carry, r=r):
            at = pl.ds(pl.multiple_of(i * ROWS, ROWS), ROWS)
            probs = jnp.exp(s_buf[at, :] * jnp.float32(scaling) - rows_buf[r + 1 : r + 2, :])
            if r == 0:
                probs = jnp.where(spread >= i * ROWS, probs, jnp.float32(0.0))
            if r == 3:
                probs = jnp.where(spread < i * ROWS + tok // 2, probs, jnp.float32(0.0))
            dropped = probs * kept[r, at, :]
            pk_buf[at, :] = dropped.astype(jnp.bfloat16)
            ds_buf[at, :] = (dropped * dp_buf[at, :] - probs * rows_buf[0:1, :]).astype(
                jnp.bfloat16
            )
            return carry

        lax.fori_loop(0, tok // ROWS, pair_rows, 0)
        add_value = dot(pk_buf[...], g_st[...], NN) * jnp.float32(keep_scale)
        add_key = dot(ds_buf[...], q_st[...], NN) * jnp.float32(keep_scale * scaling)
        if r > 0:
            back_out[r - 1, 0] = add_key.astype(jnp.bfloat16)
            back_out[r - 1, 1] = add_value.astype(jnp.bfloat16)
            for part in range(2):
                copy = pltpu.make_async_remote_copy(
                    src_ref=back_out.at[r - 1, part],
                    dst_ref=back_in.at[r - 1, part],
                    send_sem=back_send.at[r - 1, part],
                    recv_sem=back_recv.at[r - 1, part],
                    device_id=(ctx_at(-r), group_id),
                    device_id_type=MESH,
                )
                copy.start()
                back_copies[r, part] = copy
        else:
            own_acc[0] = add_key
            own_acc[1] = add_value
        add_query = dot(key_blk[...], ds_buf[...], TN)
        if place == 0:
            dq_acc[...] = add_query
        else:
            dq_acc[...] += add_query

    for h in range(heads):
        part_t = jnp.transpose(dq_acc[:, pl.ds(h * tok, tok)])
        grads[:, pl.ds(h * hd, hd)] = (part_t * jnp.float32(keep_scale * scaling)).astype(
            jnp.bfloat16
        )

    for copy in weight_loads:
        copy.wait()

    def query_terms(i, carry):
        at = pl.ds(pl.multiple_of(i * tok, tok), tok)
        terms[i] = dot(grads[...], wq[at, :], NT)
        return carry

    lax.fori_loop(0, 16, query_terms, 0)

    for r in (2, 1, 3):
        for part in range(2):
            back_copies[r, part].wait_recv()
    for part in range(2):
        total = own_acc[part]
        for r in (1, 2, 3):
            total = total + back_in[r - 1, part].astype(jnp.float32)
        kv_grads[:, pl.ds(part * hd, hd)] = total.astype(jnp.bfloat16)

    def term(index):
        at = pl.ds(pl.multiple_of(index * tok, tok), tok)
        return terms[index] + dot(kv_grads[...], wkv[at, :], NT)

    pair_copies = []

    def send_pair(j):
        pair_out[j] = term(chip_at(HOPS[j]) * 2 + 1 - core).astype(jnp.bfloat16)
        copy = pltpu.make_async_remote_copy(
            src_ref=pair_out.at[j],
            dst_ref=pair_in.at[j],
            send_sem=pair_send.at[j],
            recv_sem=pair_recv.at[j],
            device_id=(block_id, partner),
            device_id_type=MESH,
        )
        copy.start()
        pair_copies.append(copy)

    far_copies = []
    send_pair(0)
    send_pair(1)
    for j in range(8):
        if j + 2 < 8:
            send_pair(j + 2)
        index = chip_at(HOPS[j]) * 2 + core
        own = term(index)
        pair_copies[j].wait_recv()
        own = own + pair_in[j].astype(jnp.float32)
        if j < 7:
            far_out[j] = own.astype(jnp.bfloat16)
            copy = pltpu.make_async_remote_copy(
                src_ref=far_out.at[j],
                dst_ref=far_in.at[j],
                send_sem=far_send.at[j],
                recv_sem=far_recv.at[j],
                device_id=(block_id, index),
                device_id_type=MESH,
            )
            copy.start()
            far_copies.append(copy)
        else:
            terms[0] = own

    for copy in far_copies:
        copy.wait_recv()

    def last_rows(i, carry):
        at = pl.ds(pl.multiple_of(i * ROWS, ROWS), ROWS)
        total = terms[0, at, :]
        for j in range(7):
            total = total + far_in[j, at, :].astype(jnp.float32)
        out_ref[at, :] = total.astype(jnp.bfloat16)
        return carry

    lax.fori_loop(0, tok // ROWS, last_rows, 0)

    for copy in list(kv_copies.values()) + list(back_copies.values()) + pair_copies + far_copies:
        copy.wait_send()


def on_device(*args):
    queries, keys, values, outputs, out_grad, log_norm = args[:6]
    block_mask, counter_base, q_weight, k_weight, v_weight = args[6:]
    tok, hd = keys.shape
    heads = log_norm.shape[1]
    wide = heads * tok
    width = q_weight.shape[0]
    any_spec = pl.BlockSpec(memory_space=pl.ANY)
    smem_spec = pl.BlockSpec(memory_space=pltpu.SMEM)
    bf16, f32 = jnp.bfloat16, jnp.float32
    dma = pltpu.SemaphoreType.DMA
    return pl.pallas_call(
        kernel,
        out_shape=jax.ShapeDtypeStruct((tok, width // 16), bf16),
        in_specs=[any_spec] * 6 + [smem_spec] * 2 + [any_spec] * 3,
        out_specs=pl.BlockSpec(memory_space=pltpu.VMEM),
        scratch_shapes=[
            pltpu.VMEM((wide, hd), bf16),
            pltpu.VMEM((wide, hd), bf16),
            pltpu.VMEM((wide, hd), bf16),
            pltpu.VMEM((tok, heads), f32),
            pltpu.VMEM((2, tok, hd), bf16),
            pltpu.VMEM((3, 2, tok, hd), bf16),
            pltpu.VMEM((4, tok, wide), f32),
            pltpu.VMEM((tok, wide), f32),
            pltpu.VMEM((tok, wide), f32),
            pltpu.VMEM((tok, wide), bf16),
            pltpu.VMEM((tok, wide), bf16),
            pltpu.VMEM((8, wide), f32),
            pltpu.VMEM((hd, wide), f32),
            pltpu.VMEM((2, tok, hd), f32),
            pltpu.VMEM((3, 2, tok, hd), bf16),
            pltpu.VMEM((3, 2, tok, hd), bf16),
            pltpu.VMEM((tok, heads * hd), bf16),
            pltpu.VMEM((tok, 2 * hd), bf16),
            pltpu.VMEM((width, heads * hd), bf16),
            pltpu.VMEM((width, 2 * hd), bf16),
            pltpu.VMEM((16, tok, width // 16), f32),
            pltpu.VMEM((8, tok, width // 16), bf16),
            pltpu.VMEM((8, tok, width // 16), bf16),
            pltpu.VMEM((7, tok, width // 16), bf16),
            pltpu.VMEM((7, tok, width // 16), bf16),
            dma((2 + 3 * heads + 1 + 3,)),
            dma((3, 2)),
            dma((3, 2)),
            dma((3, 2)),
            dma((3, 2)),
            dma((8,)),
            dma((8,)),
            dma((7,)),
            dma((7,)),
        ],
        compiler_params=pltpu.CompilerParams(
            collective_id=0,
            has_side_effects=True,
            vmem_limit_bytes=58 * 1024 * 1024,
        ),
    )(*args)


def solution(mesh):
    return jax.shard_map(
        on_device,
        mesh=mesh,
        in_specs=(
            P("ctx", "tp"),
            P("ctx", "tp"),
            P("ctx", "tp"),
            P("ctx", "tp"),
            P("ctx", "tp"),
            P("ctx", "tp"),
            P("ctx", None),
            P(),
            P(None, "tp"),
            P(None, "tp"),
            P(None, "tp"),
        ),
        out_specs=P("ctx", "tp"),
        check_vma=False,
    )
```

time: 234 us -> 64.1 us (0.27)
  waiting for transfers between devices: 135 us -> 0 us
  Pallas kernels: 0 us -> 60.7 us
  starting transfers between devices: 51.7 us -> 0 us
  matrix products: 19.2 us -> 0 us
  between operations: 16.7 us -> 0.01 us
  other arithmetic: 4.11 us -> 0 us
  local copies, waits for them, and re-layouts: 5.55 us -> 3.05 us
    reduce_scatter x1 -> x0, waiting for transfers between devices: 127 us -> none  [on_device(): lax.psum_scatter(partial_term.astype(jnp.bfloat16), 'tp', scatter_dimensi...]
    pallas_call x0 -> x1, Pallas kernels: none -> 60.7 us  [on_device(): pl.pallas_call(kernel, out_shape=jax.ShapeDtypeStruct((tok, width // 16),...]
    ppermute x14 -> x0, starting transfers between devices: 51.7 us -> none  [the longest x8 32.8 us: passed_along(): return lax.ppermute(value, axis, pairs)]
    dot_general x23 -> x0, matrix products: 19.2 us -> none  [the longest x4 5.41 us: pair_grads(): jnp.einsum('qhd,kd->hqk', grad_out, value_blk, preferred_element_type=jnp...]
    ppermute x14 -> x0, waiting for transfers between devices: 8.28 us -> none  [the longest x8 6 us: passed_along(): return lax.ppermute(value, axis, pairs)]
    slice x2 -> x0, local copies, waits for them, and re-layouts: 2.8 us -> none  [the longest x1 1.48 us: on_device(): active = (source >= 0) & (mask_row[offset] == 1)]
    mul x5 -> x0, other arithmetic: 2.61 us -> none  [the longest x3 1.96 us: keep_mask(): key_pos[None, None, :] * 19349663]
    unnamed x16 -> x2, local copies, waits for them, and re-layouts: 0.5 us -> 3.05 us
  transfers between devices with their start and end apart: 15 -> 0, of which waited for: 5 -> 0; matrix products, arithmetic and copies ran while one was open for 11% -> 0% of each run, Pallas kernels for 0% -> 0%
where the time goes in v1:
time: 64.1 us; the launch traced here: 63.7 us
  Pallas kernels  60.7 us (95%)
  local copies, waits for them, and re-layouts  3.05 us (5%)
    pallas_call x1, Pallas kernels, on_device(): pl.pallas_call(kernel, out_shape=jax.ShapeDtypeStruct((tok, width // 16),...  60.7 us
    unnamed x2, local copies, waits for them, and re-layouts  3.05 us

profile of v1, /device:TPU:1, one launch (start us, length us, event | category | flops | bytes accessed | tf_op | source)
XLA Modules:
  0.0 63.7 jit_solution(7590649486390613792)
XLA Ops:
  0.0 1.5 %copy.12.norm_hbm = f32[256,4]{1,0:T(8,128)} copy(f32[256,4]{0,1:T(4,128)} %param.16) | data formatting | bytes 8192 | tf_op args[5]
  1.5 60.7 %shard_map.109 = bf16[256,256]{1,0:T(8,128)(2,1)} custom-call(bf16[256,512]{1,0:T(8,128)(2,1)} %q_hbm.1, bf16[256,128]{1,0:T(8,128)(2,1)} %k_hbm.1, bf16[256,128]{1,0:T(8,128)(2,1)} %v_hbm.1, bf16[256,512]{1,0:T(8,128)(2,1)} %o_hbm.1, bf16[256,512]{1,0:T(8,128)(2,1)} %g_hbm.1, f32[256,4]{1,0:T(8,128)} %copy.12.norm_hbm, s32[1,4]{1,0:T(1,128)} %mask_smem.1, ...), custom_call_target="tpu_custom_call" | custom-call | tf_op jit(solution)/shard_map/pallas_call | solution.py:339
  62.2 1.6 %copy.14 = bf16[256,256]{1,0:T(8,128)(2,1)} copy(bf16[256,256]{1,0:T(8,128)(2,1)} %shard_map.109) | data formatting | bytes 262144

commit v2 on v1

--- a/solution.py
+++ b/solution.py
@@ -14,7 +14,7 @@
 NT = (((1,), (1,)), ((), ()))
 NN = (((1,), (0,)), ((), ()))
 TN = (((0,), (0,)), ((), ()))
-HOPS = ((2, 1), (2, 0), (1, 1), (3, 1), (0, 1), (1, 0), (3, 0), (0, 0))
+HOPS = ((2, 1), (1, 1), (3, 1), (0, 1), (2, 0), (1, 0), (3, 0), (0, 0))
 OFFSETS = (2, 1, 3, 0)
 
 
@@ -56,6 +56,7 @@
     wq,
     wkv,
     terms,
+    sums,
     pair_out,
     pair_in,
     far_out,
@@ -89,6 +90,8 @@
         return lax.rem(y_pos + hop[0], 4) * 2 + lax.rem(x_pos + hop[1], 2)
 
     partner = group_id + 1 - 2 * core
+    parity = block_id % 2
+    x_peer = block_id + 1 - 2 * parity
 
     loads = []
 
@@ -115,28 +118,32 @@
     barrier = pltpu.get_barrier_semaphore()
     peers = [(ctx_at(r), group_id) for r in (1, -1, 2, -2, 3, -3)]
     peers.append((block_id, partner))
-    peers += [(block_id, chip_at(hop) * 2 + core) for hop in HOPS[:-1]]
+    peers += [(block_id, chip_at(hop) * 2 + core) for hop in HOPS[3:7]]
     for peer in peers:
         pl.semaphore_signal(barrier, inc=1, device_id=peer, device_id_type=MESH)
     pl.semaphore_wait(barrier, len(peers))
 
     for copy in kv_loads:
         copy.wait()
-    kv_copies = {}
-    for r in (1, 2, 3):
-        for part in range(2):
-            copy = pltpu.make_async_remote_copy(
-                src_ref=own_kv.at[part],
-                dst_ref=got_kv.at[r - 1, part],
-                send_sem=kv_send.at[r - 1, part],
-                recv_sem=kv_recv.at[r - 1, part],
-                device_id=(ctx_at(r), group_id),
-                device_id_type=MESH,
-            )
-            kv_copies[r, part] = copy
-    for r in (2, 1, 3):
-        for part in range(2):
-            kv_copies[r, part].start()
+    def kv_copy(r, part, src):
+        return pltpu.make_async_remote_copy(
+            src_ref=src.at[part],
+            dst_ref=got_kv.at[r - 1, part],
+            send_sem=kv_send.at[r - 1, part],
+            recv_sem=kv_recv.at[r - 1, part],
+            device_id=(x_peer if r == 1 else ctx_at(2), group_id),
+            device_id_type=MESH,
+        )
+
+    def kv_wait(r, part):
+        kv_copy(r, part, own_kv).wait_recv()
+
+    for part in range(2):
+        kv_copy(2, part, own_kv).start()
+
+        @pl.when(parity == 0)
+        def _():
+            kv_copy(1, part, own_kv).start()
 
     lane = lax.broadcasted_iota(jnp.int32, (ROWS, wide), 1)
     sub = lax.broadcasted_iota(jnp.int32, (ROWS, wide), 0)
@@ -179,18 +186,39 @@
         prod = g_st[rows, :].astype(jnp.float32) * o_st[rows, :].astype(jnp.float32)
         delta = jnp.sum(jnp.transpose(prod), axis=0, keepdims=True)
         rows_buf[0:1, rows] = delta * jnp.float32(1.0 / keep_scale)
-        column = jnp.broadcast_to(norm_in[:, h : h + 1], (tok, hd))
-        norm_row = jnp.transpose(column)[0:1, :]
         for r in range(4):
             active = (block_id - r >= 0) & (mask_smem[0, r] == 1)
             push = jnp.where(active, jnp.float32(0.0), jnp.float32(1e30))
-            rows_buf[r + 1 : r + 2, rows] = norm_row + push
+            rows_buf[r + 1 : r + 2, rows] = norm_in[h : h + 1, :] + push
+
+    def pass_on():
+        for part in range(2):
+            kv_wait(1, part)
+            kv_copy(3, part, got_kv.at[0]).start()
+
+    for part in range(2):
+        kv_wait(2, part)
+
+        @pl.when(parity == 1)
+        def _():
+            kv_copy(1, part, got_kv.at[1]).start()
+
+    @pl.when(parity == 1)
+    def _():
+        pass_on()
 
     back_copies = {}
     for place, r in enumerate(OFFSETS):
+        if r == 1:
+
+            @pl.when(parity == 0)
+            def _():
+                pass_on()
+
+        if r == 3:
+            for part in range(2):
+                kv_wait(3, part)
         if r > 0:
-            for part in range(2):
-                kv_copies[r, part].wait_recv()
             key_blk = got_kv.at[r - 1, 0]
             value_blk = got_kv.at[r - 1, 1]
         else:
@@ -283,51 +311,78 @@
         copy.start()
         pair_copies.append(copy)
 
-    far_copies = []
+    def far_copy(j):
+        if j < 3:
+            hop_y, hop_x = core * HOPS[j][0], 1 - core
+        else:
+            hop_y, hop_x = HOPS[j][0], HOPS[j][1]
+        return pltpu.make_async_remote_copy(
+            src_ref=far_out.at[j],
+            dst_ref=far_in.at[j],
+            send_sem=far_send.at[j],
+            recv_sem=far_recv.at[j],
+            device_id=(block_id, chip_at((hop_y, hop_x)) * 2 + core),
+            device_id_type=MESH,
+        )
+
+    def send_far(j, value):
+        far_out[j] = value.astype(jnp.bfloat16)
+        far_copy(j).start()
+
     send_pair(0)
     send_pair(1)
     for j in range(8):
         if j + 2 < 8:
             send_pair(j + 2)
-        index = chip_at(HOPS[j]) * 2 + core
-        own = term(index)
+        own = term(chip_at(HOPS[j]) * 2 + core)
         pair_copies[j].wait_recv()
         own = own + pair_in[j].astype(jnp.float32)
-        if j < 7:
-            far_out[j] = own.astype(jnp.bfloat16)
-            copy = pltpu.make_async_remote_copy(
-                src_ref=far_out.at[j],
-                dst_ref=far_in.at[j],
-                send_sem=far_send.at[j],
-                recv_sem=far_recv.at[j],
-                device_id=(block_id, index),
-                device_id_type=MESH,
-            )
-            copy.start()
-            far_copies.append(copy)
+        if j < 3:
+            send_far(j, own)
         else:
-            terms[0] = own
-
-    for copy in far_copies:
-        copy.wait_recv()
+            sums[j - 3] = own
+        if 3 <= j < 7:
+
+            @pl.when(core == (0 if j == 3 else 1))
+            def _():
+                send_far(j, sums[j - 3])
+
+    @pl.when(core == 0)
+    def _():
+        for j in range(3):
+            far_copy(j).wait_recv()
+            send_far(j + 4, sums[j + 1] + far_in[j].astype(jnp.float32))
+
+    @pl.when(core == 1)
+    def _():
+        total = sums[0]
+        for j in range(3):
+            far_copy(j).wait_recv()
+            total = total + far_in[j].astype(jnp.float32)
+        send_far(3, total)
+
+    for j in (4, 5, 6, 3):
+        far_copy(j).wait_recv()
 
     def last_rows(i, carry):
         at = pl.ds(pl.multiple_of(i * ROWS, ROWS), ROWS)
-        total = terms[0, at, :]
-        for j in range(7):
+        total = sums[4, at, :]
+        for j in range(3, 7):
             total = total + far_in[j, at, :].astype(jnp.float32)
-        out_ref[at, :] = total.astype(jnp.bfloat16)
+        out_ref[at, :] = total
         return carry
 
     lax.fori_loop(0, tok // ROWS, last_rows, 0)
 
-    for copy in list(kv_copies.values()) + list(back_copies.values()) + pair_copies + far_copies:
+    sent = [kv_copy(r, part, own_kv) for r in (1, 2, 3) for part in range(2)]
+    sent += list(back_copies.values()) + pair_copies + [far_copy(j) for j in range(7)]
+    for copy in sent:
         copy.wait_send()
 
 
 def on_device(*args):
     queries, keys, values, outputs, out_grad, log_norm = args[:6]
-    block_mask, counter_base, q_weight, k_weight, v_weight = args[6:]
+    q_weight = args[8]
     tok, hd = keys.shape
     heads = log_norm.shape[1]
     wide = heads * tok
@@ -336,16 +391,16 @@
     smem_spec = pl.BlockSpec(memory_space=pltpu.SMEM)
     bf16, f32 = jnp.bfloat16, jnp.float32
     dma = pltpu.SemaphoreType.DMA
-    return pl.pallas_call(
+    total = pl.pallas_call(
         kernel,
-        out_shape=jax.ShapeDtypeStruct((tok, width // 16), bf16),
+        out_shape=jax.ShapeDtypeStruct((tok, width // 16), f32),
         in_specs=[any_spec] * 6 + [smem_spec] * 2 + [any_spec] * 3,
         out_specs=pl.BlockSpec(memory_space=pltpu.VMEM),
         scratch_shapes=[
             pltpu.VMEM((wide, hd), bf16),
             pltpu.VMEM((wide, hd), bf16),
             pltpu.VMEM((wide, hd), bf16),
-            pltpu.VMEM((tok, heads), f32),
+            pltpu.VMEM((heads, tok), f32),
             pltpu.VMEM((2, tok, hd), bf16),
             pltpu.VMEM((3, 2, tok, hd), bf16),
             pltpu.VMEM((4, tok, wide), f32),
@@ -363,6 +418,7 @@
             pltpu.VMEM((width, heads * hd), bf16),
             pltpu.VMEM((width, 2 * hd), bf16),
             pltpu.VMEM((16, tok, width // 16), f32),
+            pltpu.VMEM((5, tok, width // 16), f32),
             pltpu.VMEM((8, tok, width // 16), bf16),
             pltpu.VMEM((8, tok, width // 16), bf16),
             pltpu.VMEM((7, tok, width // 16), bf16),
@@ -382,7 +438,8 @@
             has_side_effects=True,
             vmem_limit_bytes=58 * 1024 * 1024,
         ),
-    )(*args)
+    )(queries, keys, values, outputs, out_grad, log_norm.T, *args[6:])
+    return total.astype(bf16)
 
 
 def solution(mesh):

time: 64.1 us -> 55.5 us (0.87)
  Pallas kernels: 60.7 us -> 53.7 us
  local copies, waits for them, and re-layouts: 3.05 us -> 0 us
  other arithmetic: 0 us -> 1.62 us
    pallas_call x1, Pallas kernels: 60.7 us -> 53.7 us  [on_device(): pl.pallas_call(kernel, out_shape=jax.ShapeDtypeStruct((tok, width // 16),...]
    unnamed x2 -> x0, local copies, waits for them, and re-layouts: 3.05 us -> none
    convert_element_type x0 -> x1, other arithmetic: none -> 1.62 us  [on_device(): return total.astype(bf16)]
where the time goes in v2:
time: 55.5 us; the launch traced here: 55.3 us
  Pallas kernels  53.7 us (97%)
  other arithmetic  1.62 us (3%)
    pallas_call x1, Pallas kernels, on_device(): pl.pallas_call(kernel, out_shape=jax.ShapeDtypeStruct((tok, width // 16),...  53.7 us
    convert_element_type x1, other arithmetic, on_device(): return total.astype(bf16)  1.62 us

profile of v2, /device:TPU:1, one launch (start us, length us, event | category | flops | bytes accessed | tf_op | source)
XLA Modules:
  0.0 55.3 jit_solution(736119832294700848)
XLA Ops:
  0.0 53.7 %shard_map.109 = f32[256,256]{1,0:T(8,128)} custom-call(bf16[256,512]{1,0:T(8,128)(2,1)} %q_hbm.1, bf16[256,128]{1,0:T(8,128)(2,1)} %k_hbm.1, bf16[256,128]{1,0:T(8,128)(2,1)} %v_hbm.1, bf16[256,512]{1,0:T(8,128)(2,1)} %o_hbm.1, bf16[256,512]{1,0:T(8,128)(2,1)} %g_hbm.1, f32[4,256]{1,0:T(4,128)} %bitcast.1, s32[1,4]{1,0:T(1,128)} %mask_smem.1, s32[2]{0:T(128)} %base_smem.1, ...), custom_call_target="tpu_custom_call" | custom-call | tf_op jit(solution)/shard_map/pallas_call | solution.py:394
  53.7 1.6 %convert_element_type.3 = bf16[256,256]{1,0:T(8,128)(2,1)} convert(f32[256,256]{1,0:T(8,128)} %shard_map.109) | non-fusion elementwise | flops 65536 | bytes 393216 | tf_op jit(solution)/shard_map/convert_element_type | solution.py:442

commit v3 on v2

--- a/solution.py
+++ b/solution.py
@@ -75,6 +75,8 @@
     hd = k_hbm.shape[1]
     heads = q_hbm.shape[1] // hd
     wide = heads * tok
+    half_rows = tok // 2
+    halves = [pl.ds(half * half_rows, half_rows) for half in range(2)]
     blocks = lax.axis_size("ctx")
     block_id = lax.axis_index("ctx")
     group_id = lax.axis_index("tp")
@@ -241,26 +243,27 @@
             )
             return carry
 
-        lax.fori_loop(0, tok // ROWS, pair_rows, 0)
-        add_value = dot(pk_buf[...], g_st[...], NN) * jnp.float32(keep_scale)
-        add_key = dot(ds_buf[...], q_st[...], NN) * jnp.float32(keep_scale * scaling)
-        if r > 0:
-            back_out[r - 1, 0] = add_key.astype(jnp.bfloat16)
-            back_out[r - 1, 1] = add_value.astype(jnp.bfloat16)
-            for part in range(2):
+        for half, at in enumerate(halves):
+            steps = half_rows // ROWS
+            lax.fori_loop(half * steps, (half + 1) * steps, pair_rows, 0)
+            add_key = dot(ds_buf[at, :], q_st[...], NN) * jnp.float32(keep_scale * scaling)
+            add_value = dot(pk_buf[at, :], g_st[...], NN) * jnp.float32(keep_scale)
+            if r > 0:
+                back_out[r - 1, half, :, 0:hd] = add_key.astype(jnp.bfloat16)
+                back_out[r - 1, half, :, hd : 2 * hd] = add_value.astype(jnp.bfloat16)
                 copy = pltpu.make_async_remote_copy(
-                    src_ref=back_out.at[r - 1, part],
-                    dst_ref=back_in.at[r - 1, part],
-                    send_sem=back_send.at[r - 1, part],
-                    recv_sem=back_recv.at[r - 1, part],
+                    src_ref=back_out.at[r - 1, half],
+                    dst_ref=back_in.at[r - 1, half],
+                    send_sem=back_send.at[r - 1, half],
+                    recv_sem=back_recv.at[r - 1, half],
                     device_id=(ctx_at(-r), group_id),
                     device_id_type=MESH,
                 )
                 copy.start()
-                back_copies[r, part] = copy
-        else:
-            own_acc[0] = add_key
-            own_acc[1] = add_value
+                back_copies[r, half] = copy
+            else:
+                own_acc[at, 0:hd] = add_key
+                own_acc[at, hd : 2 * hd] = add_value
         add_query = dot(key_blk[...], ds_buf[...], TN)
         if place == 0:
             dq_acc[...] = add_query
@@ -283,99 +286,111 @@
 
     lax.fori_loop(0, 16, query_terms, 0)
 
-    for r in (2, 1, 3):
-        for part in range(2):
-            back_copies[r, part].wait_recv()
-    for part in range(2):
-        total = own_acc[part]
-        for r in (1, 2, 3):
-            total = total + back_in[r - 1, part].astype(jnp.float32)
-        kv_grads[:, pl.ds(part * hd, hd)] = total.astype(jnp.bfloat16)
-
-    def term(index):
+    def term(index, half):
         at = pl.ds(pl.multiple_of(index * tok, tok), tok)
-        return terms[index] + dot(kv_grads[...], wkv[at, :], NT)
-
-    pair_copies = []
-
-    def send_pair(j):
-        pair_out[j] = term(chip_at(HOPS[j]) * 2 + 1 - core).astype(jnp.bfloat16)
+        return terms[index, halves[half], :] + dot(kv_grads[halves[half], :], wkv[at, :], NT)
+
+    pair_copies = {}
+
+    def send_pair(j, half):
+        value = term(chip_at(HOPS[j]) * 2 + 1 - core, half)
+        pair_out[half, j] = value.astype(jnp.bfloat16)
         copy = pltpu.make_async_remote_copy(
-            src_ref=pair_out.at[j],
-            dst_ref=pair_in.at[j],
-            send_sem=pair_send.at[j],
-            recv_sem=pair_recv.at[j],
+            src_ref=pair_out.at[half, j],
+            dst_ref=pair_in.at[half, j],
+            send_sem=pair_send.at[half, j],
+            recv_sem=pair_recv.at[half, j],
             device_id=(block_id, partner),
             device_id_type=MESH,
         )
         copy.start()
-        pair_copies.append(copy)
-
-    def far_copy(j):
+        pair_copies[j, half] = copy
+
+    def far_copy(j, half):
         if j < 3:
             hop_y, hop_x = core * HOPS[j][0], 1 - core
         else:
             hop_y, hop_x = HOPS[j][0], HOPS[j][1]
         return pltpu.make_async_remote_copy(
-            src_ref=far_out.at[j],
-            dst_ref=far_in.at[j],
-            send_sem=far_send.at[j],
-            recv_sem=far_recv.at[j],
+            src_ref=far_out.at[half, j],
+            dst_ref=far_in.at[half, j],
+            send_sem=far_send.at[half, j],
+            recv_sem=far_recv.at[half, j],
             device_id=(block_id, chip_at((hop_y, hop_x)) * 2 + core),
             device_id_type=MESH,
         )
 
-    def send_far(j, value):
-        far_out[j] = value.astype(jnp.bfloat16)
-        far_copy(j).start()
-
-    send_pair(0)
-    send_pair(1)
-    for j in range(8):
-        if j + 2 < 8:
-            send_pair(j + 2)
-        own = term(chip_at(HOPS[j]) * 2 + core)
-        pair_copies[j].wait_recv()
-        own = own + pair_in[j].astype(jnp.float32)
-        if j < 3:
-            send_far(j, own)
-        else:
-            sums[j - 3] = own
-        if 3 <= j < 7:
-
-            @pl.when(core == (0 if j == 3 else 1))
-            def _():
-                send_far(j, sums[j - 3])
-
-    @pl.when(core == 0)
-    def _():
-        for j in range(3):
-            far_copy(j).wait_recv()
-            send_far(j + 4, sums[j + 1] + far_in[j].astype(jnp.float32))
-
-    @pl.when(core == 1)
-    def _():
-        total = sums[0]
-        for j in range(3):
-            far_copy(j).wait_recv()
-            total = total + far_in[j].astype(jnp.float32)
-        send_far(3, total)
-
-    for j in (4, 5, 6, 3):
-        far_copy(j).wait_recv()
-
-    def last_rows(i, carry):
-        at = pl.ds(pl.multiple_of(i * ROWS, ROWS), ROWS)
-        total = sums[4, at, :]
-        for j in range(3, 7):
-            total = total + far_in[j, at, :].astype(jnp.float32)
-        out_ref[at, :] = total
-        return carry
-
-    lax.fori_loop(0, tok // ROWS, last_rows, 0)
+    def send_far(j, half, value):
+        far_out[half, j] = value.astype(jnp.bfloat16)
+        far_copy(j, half).start()
+
+    def first_phase(half):
+        at = halves[half]
+        for r in (2, 1, 3):
+            back_copies[r, half].wait_recv()
+        total = own_acc[at, :]
+        for r in (1, 2, 3):
+            total = total + back_in[r - 1, half].astype(jnp.float32)
+        kv_grads[at, :] = total.astype(jnp.bfloat16)
+        send_pair(0, half)
+        send_pair(1, half)
+        for j in range(8):
+            if j + 2 < 8:
+                send_pair(j + 2, half)
+            own = term(chip_at(HOPS[j]) * 2 + core, half)
+            pair_copies[j, half].wait_recv()
+            own = own + pair_in[half, j].astype(jnp.float32)
+            if j < 3:
+                send_far(j, half, own)
+            else:
+                sums[j - 3, at, :] = own
+            if 3 <= j < 7:
+
+                @pl.when(core == (0 if j == 3 else 1))
+                def _():
+                    send_far(j, half, sums[j - 3, at, :])
+
+    def second_phase(half):
+        at = halves[half]
+
+        @pl.when(core == 0)
+        def _():
+            for j in range(3):
+                far_copy(j, half).wait_recv()
+                value = sums[j + 1, at, :] + far_in[half, j].astype(jnp.float32)
+                send_far(j + 4, half, value)
+
+        @pl.when(core == 1)
+        def _():
+            total = sums[0, at, :]
+            for j in range(3):
+                far_copy(j, half).wait_recv()
+                total = total + far_in[half, j].astype(jnp.float32)
+            send_far(3, half, total)
+
+    first_phase(0)
+    first_phase(1)
+    second_phase(0)
+    second_phase(1)
+
+    for half in range(2):
+        for j in (4, 5, 6, 3):
+            far_copy(j, half).wait_recv()
+
+        def last_rows(i, carry, half=half):
+            at = pl.ds(pl.multiple_of(i * ROWS, ROWS), ROWS)
+            all_at = pl.ds(pl.multiple_of(i * ROWS + half * half_rows, ROWS), ROWS)
+            total = sums[4, all_at, :]
+            for j in range(3, 7):
+                total = total + far_in[half, j, at, :].astype(jnp.float32)
+            out_ref[all_at, :] = total
+            return carry
+
+        lax.fori_loop(0, half_rows // ROWS, last_rows, 0)
 
     sent = [kv_copy(r, part, own_kv) for r in (1, 2, 3) for part in range(2)]
-    sent += list(back_copies.values()) + pair_copies + [far_copy(j) for j in range(7)]
+    sent += list(back_copies.values()) + list(pair_copies.values())
+    sent += [far_copy(j, half) for half in range(2) for j in range(7)]
     for copy in sent:
         copy.wait_send()
 
@@ -391,6 +406,8 @@
     smem_spec = pl.BlockSpec(memory_space=pltpu.SMEM)
     bf16, f32 = jnp.bfloat16, jnp.float32
     dma = pltpu.SemaphoreType.DMA
+    operands = (queries, keys, values, outputs, out_grad, log_norm.T, *args[6:])
+    held = [pltpu.with_memory_space_constraint(x, pltpu.HBM) for x in operands]
     total = pl.pallas_call(
         kernel,
         out_shape=jax.ShapeDtypeStruct((tok, width // 16), f32),
@@ -410,35 +427,35 @@
             pltpu.VMEM((tok, wide), bf16),
             pltpu.VMEM((8, wide), f32),
             pltpu.VMEM((hd, wide), f32),
-            pltpu.VMEM((2, tok, hd), f32),
-            pltpu.VMEM((3, 2, tok, hd), bf16),
-            pltpu.VMEM((3, 2, tok, hd), bf16),
+            pltpu.VMEM((tok, 2 * hd), f32),
+            pltpu.VMEM((3, 2, tok // 2, 2 * hd), bf16),
+            pltpu.VMEM((3, 2, tok // 2, 2 * hd), bf16),
             pltpu.VMEM((tok, heads * hd), bf16),
             pltpu.VMEM((tok, 2 * hd), bf16),
             pltpu.VMEM((width, heads * hd), bf16),
             pltpu.VMEM((width, 2 * hd), bf16),
             pltpu.VMEM((16, tok, width // 16), f32),
             pltpu.VMEM((5, tok, width // 16), f32),
-            pltpu.VMEM((8, tok, width // 16), bf16),
-            pltpu.VMEM((8, tok, width // 16), bf16),
-            pltpu.VMEM((7, tok, width // 16), bf16),
-            pltpu.VMEM((7, tok, width // 16), bf16),
+            pltpu.VMEM((2, 8, tok // 2, width // 16), bf16),
+            pltpu.VMEM((2, 8, tok // 2, width // 16), bf16),
+            pltpu.VMEM((2, 7, tok // 2, width // 16), bf16),
+            pltpu.VMEM((2, 7, tok // 2, width // 16), bf16),
             dma((2 + 3 * heads + 1 + 3,)),
             dma((3, 2)),
             dma((3, 2)),
             dma((3, 2)),
             dma((3, 2)),
-            dma((8,)),
-            dma((8,)),
-            dma((7,)),
-            dma((7,)),
+            dma((2, 8)),
+            dma((2, 8)),
+            dma((2, 7)),
+            dma((2, 7)),
         ],
         compiler_params=pltpu.CompilerParams(
             collective_id=0,
             has_side_effects=True,
-            vmem_limit_bytes=58 * 1024 * 1024,
+            vmem_limit_bytes=40 * 1024 * 1024,
         ),
-    )(queries, keys, values, outputs, out_grad, log_norm.T, *args[6:])
+    )(*held)
     return total.astype(bf16)
 
 

time: 55.5 us -> 56.1 us (1.011)
  Pallas kernels: 53.7 us -> 55.3 us
  other arithmetic: 1.62 us -> 0.67 us
    pallas_call x1, Pallas kernels: 53.7 us -> 55.3 us  [on_device(): pl.pallas_call(kernel, out_shape=jax.ShapeDtypeStruct((tok, width // 16),...]
    convert_element_type x1, other arithmetic: 1.62 us -> 0.67 us  [on_device(): return total.astype(bf16)]
where the time goes in v3:
time: 56.1 us; the launch traced here: 56 us
  Pallas kernels  55.3 us (99%)
  other arithmetic  0.67 us (1%)
    pallas_call x1, Pallas kernels, on_device(): pl.pallas_call(kernel, out_shape=jax.ShapeDtypeStruct((tok, width // 16),...  55.3 us

profile of v3, /device:TPU:1, one launch (start us, length us, event | category | flops | bytes accessed | tf_op | source)
XLA Modules:
  0.0 56.0 jit_solution(7693570017558534926)
XLA Ops:
  0.0 55.3 %shard_map.109 = f32[256,256]{1,0:T(8,128)S(1)} custom-call(bf16[256,512]{1,0:T(8,128)(2,1)} %q_hbm.1, bf16[256,128]{1,0:T(8,128)(2,1)} %k_hbm.1, bf16[256,128]{1,0:T(8,128)(2,1)} %v_hbm.1, bf16[256,512]{1,0:T(8,128)(2,1)} %o_hbm.1, bf16[256,512]{1,0:T(8,128)(2,1)} %g_hbm.1, f32[4,256]{1,0:T(4,128)} %bitcast.1, s32[1,4]{1,0:T(1,128)} %mask_smem.1, ...), custom_call_target="tpu_custom_call" | custom-call | tf_op jit(solution)/shard_map/pallas_call | solution.py:411
  55.3 0.7 %convert_element_type.3 = bf16[256,256]{1,0:T(8,128)(2,1)} convert(f32[256,256]{1,0:T(8,128)S(1)} %shard_map.109) | non-fusion elementwise | flops 65536 | bytes 393216 | tf_op jit(solution)/shard_map/convert_element_type | solution.py:459

commit v4 on v3

--- a/solution.py
+++ b/solution.py
@@ -15,7 +15,7 @@
 NN = (((1,), (0,)), ((), ()))
 TN = (((0,), (0,)), ((), ()))
 HOPS = ((2, 1), (1, 1), (3, 1), (0, 1), (2, 0), (1, 0), (3, 0), (0, 0))
-OFFSETS = (2, 1, 3, 0)
+OFFSETS = (2, 1, 0, 3)
 
 
 def dot(a, b, dims):
@@ -88,6 +88,12 @@
     def ctx_at(steps):
         return lax.rem(block_id + steps + blocks, blocks)
 
+    def at_least(steps):
+        return block_id >= steps
+
+    def room_for(steps):
+        return block_id + steps < blocks
+
     def chip_at(hop):
         return lax.rem(y_pos + hop[0], 4) * 2 + lax.rem(x_pos + hop[1], 2)
 
@@ -118,12 +124,24 @@
     ]
 
     barrier = pltpu.get_barrier_semaphore()
-    peers = [(ctx_at(r), group_id) for r in (1, -1, 2, -2, 3, -3)]
-    peers.append((block_id, partner))
-    peers += [(block_id, chip_at(hop) * 2 + core) for hop in HOPS[3:7]]
-    for peer in peers:
+
+    def greet(peer):
         pl.semaphore_signal(barrier, inc=1, device_id=peer, device_id_type=MESH)
-    pl.semaphore_wait(barrier, len(peers))
+
+    @pl.when(at_least(2))
+    def _():
+        greet((ctx_at(-2), group_id))
+
+    @pl.when((parity == 1) | at_least(2))
+    def _():
+        greet((x_peer, group_id))
+
+    greet((block_id, partner))
+    for hop in HOPS[3:7]:
+        greet((block_id, chip_at(hop) * 2 + core))
+    to_far = jnp.where(room_for(2), 1, 0)
+    to_near = jnp.where((parity == 0) | at_least(2), 1, 0)
+    pl.semaphore_wait(barrier, 5 + to_far + to_near)
 
     for copy in kv_loads:
         copy.wait()
@@ -141,7 +159,10 @@
         kv_copy(r, part, own_kv).wait_recv()
 
     for part in range(2):
-        kv_copy(2, part, own_kv).start()
+
+        @pl.when(room_for(2))
+        def _():
+            kv_copy(2, part, own_kv).start()
 
         @pl.when(parity == 0)
         def _():
@@ -193,30 +214,37 @@
             push = jnp.where(active, jnp.float32(0.0), jnp.float32(1e30))
             rows_buf[r + 1 : r + 2, rows] = norm_in[h : h + 1, :] + push
 
-    def pass_on():
+    @pl.when((parity == 1) & at_least(2))
+    def _():
+        for part in range(2):
+            kv_wait(2, part)
+            kv_copy(1, part, got_kv.at[1]).start()
+
+    @pl.when(at_least(1))
+    def _():
         for part in range(2):
             kv_wait(1, part)
-            kv_copy(3, part, got_kv.at[0]).start()
-
-    for part in range(2):
-        kv_wait(2, part)
-
-        @pl.when(parity == 1)
-        def _():
-            kv_copy(1, part, got_kv.at[1]).start()
-
-    @pl.when(parity == 1)
+
+            @pl.when(room_for(2))
+            def _():
+                kv_copy(3, part, got_kv.at[0]).start()
+
+    @pl.when((parity == 0) & at_least(2))
     def _():
-        pass_on()
-
-    back_copies = {}
-    for place, r in enumerate(OFFSETS):
-        if r == 1:
-
-            @pl.when(parity == 0)
-            def _():
-                pass_on()
-
+        for part in range(2):
+            kv_wait(2, part)
+
+    def back_copy(r, half):
+        return pltpu.make_async_remote_copy(
+            src_ref=back_out.at[r - 1, half],
+            dst_ref=back_in.at[r - 1, half],
+            send_sem=back_send.at[r - 1, half],
+            recv_sem=back_recv.at[r - 1, half],
+            device_id=(ctx_at(-r), group_id),
+            device_id_type=MESH,
+        )
+
+    def pair_grads(r):
         if r == 3:
             for part in range(2):
                 kv_wait(3, part)
@@ -251,24 +279,22 @@
             if r > 0:
                 back_out[r - 1, half, :, 0:hd] = add_key.astype(jnp.bfloat16)
                 back_out[r - 1, half, :, hd : 2 * hd] = add_value.astype(jnp.bfloat16)
-                copy = pltpu.make_async_remote_copy(
-                    src_ref=back_out.at[r - 1, half],
-                    dst_ref=back_in.at[r - 1, half],
-                    send_sem=back_send.at[r - 1, half],
-                    recv_sem=back_recv.at[r - 1, half],
-                    device_id=(ctx_at(-r), group_id),
-                    device_id_type=MESH,
-                )
-                copy.start()
-                back_copies[r, half] = copy
+                back_copy(r, half).start()
             else:
                 own_acc[at, 0:hd] = add_key
                 own_acc[at, hd : 2 * hd] = add_value
         add_query = dot(key_blk[...], ds_buf[...], TN)
-        if place == 0:
-            dq_acc[...] = add_query
+        dq_acc[...] += add_query
+
+    dq_acc[...] = jnp.zeros_like(dq_acc)
+    for r in OFFSETS:
+        if r == 0:
+            pair_grads(r)
         else:
-            dq_acc[...] += add_query
+
+            @pl.when(at_least(r))
+            def _():
+                pair_grads(r)
 
     for h in range(heads):
         part_t = jnp.transpose(dq_acc[:, pl.ds(h * tok, tok)])
@@ -327,11 +353,13 @@
     def first_phase(half):
         at = halves[half]
         for r in (2, 1, 3):
-            back_copies[r, half].wait_recv()
-        total = own_acc[at, :]
-        for r in (1, 2, 3):
-            total = total + back_in[r - 1, half].astype(jnp.float32)
-        kv_grads[at, :] = total.astype(jnp.bfloat16)
+
+            @pl.when(room_for(r))
+            def _():
+                back_copy(r, half).wait_recv()
+                own_acc[at, :] += back_in[r - 1, half].astype(jnp.float32)
+
+        kv_grads[at, :] = own_acc[at, :].astype(jnp.bfloat16)
         send_pair(0, half)
         send_pair(1, half)
         for j in range(8):
@@ -388,11 +416,24 @@
 
         lax.fori_loop(0, half_rows // ROWS, last_rows, 0)
 
-    sent = [kv_copy(r, part, own_kv) for r in (1, 2, 3) for part in range(2)]
-    sent += list(back_copies.values()) + list(pair_copies.values())
-    sent += [far_copy(j, half) for half in range(2) for j in range(7)]
-    for copy in sent:
-        copy.wait_send()
+    sends = (
+        (room_for(2), [kv_copy(2, part, own_kv) for part in range(2)]),
+        ((parity == 0) | at_least(2), [kv_copy(1, part, own_kv) for part in range(2)]),
+        (at_least(1) & room_for(2), [kv_copy(3, part, own_kv) for part in range(2)]),
+    )
+    sends += tuple((at_least(r), [back_copy(r, half) for half in range(2)]) for r in (1, 2, 3))
+    for sent, copies in sends:
+
+        @pl.when(sent)
+        def _():
+            for copy in copies:
+                copy.wait_send()
+
+    for half in range(2):
+        for j in range(8):
+            pair_copies[j, half].wait_send()
+        for j in range(7):
+            far_copy(j, half).wait_send()
 
 
 def on_device(*args):

time: 56.1 us -> 45.1 us (0.80)
  the two profiles are of different devices: /device:TPU:1 before, /device:TPU:450 now
where the time goes in v4:
time: 45.1 us; the launch traced here: 45 us
  Pallas kernels  44.3 us (98%)
  other arithmetic  0.67 us (1%)
    pallas_call x1, Pallas kernels, on_device(): pl.pallas_call(kernel, out_shape=jax.ShapeDtypeStruct((tok, width // 16),...  44.3 us

profile of v4, /device:TPU:450, one launch (start us, length us, event | category | flops | bytes accessed | tf_op | source)
XLA Modules:
  0.0 45.0 jit_solution(10179683044151385233)
XLA Ops:
  0.0 44.3 %shard_map.109 = f32[256,256]{1,0:T(8,128)S(1)} custom-call(bf16[256,512]{1,0:T(8,128)(2,1)} %q_hbm.1, bf16[256,128]{1,0:T(8,128)(2,1)} %k_hbm.1, bf16[256,128]{1,0:T(8,128)(2,1)} %v_hbm.1, bf16[256,512]{1,0:T(8,128)(2,1)} %o_hbm.1, bf16[256,512]{1,0:T(8,128)(2,1)} %g_hbm.1, f32[4,256]{1,0:T(4,128)} %bitcast.1, s32[1,4]{1,0:T(1,128)} %mask_smem.1, ...), custom_call_target="tpu_custom_call" | custom-call | tf_op jit(solution)/shard_map/pallas_call | solution.py:452
  44.3 0.7 %convert_element_type.3 = bf16[256,256]{1,0:T(8,128)(2,1)} convert(f32[256,256]{1,0:T(8,128)S(1)} %shard_map.109) | non-fusion elementwise | flops 65536 | bytes 393216 | tf_op jit(solution)/shard_map/convert_element_type | solution.py:500

commit v5 on v4

--- a/solution.py
+++ b/solution.py
@@ -145,10 +145,13 @@
 
     for copy in kv_loads:
         copy.wait()
+    def piece(part):
+        return part // 2, halves[part % 2]
+
     def kv_copy(r, part, src):
         return pltpu.make_async_remote_copy(
-            src_ref=src.at[part],
-            dst_ref=got_kv.at[r - 1, part],
+            src_ref=src.at[piece(part)],
+            dst_ref=got_kv.at[r - 1].at[piece(part)],
             send_sem=kv_send.at[r - 1, part],
             recv_sem=kv_recv.at[r - 1, part],
             device_id=(x_peer if r == 1 else ctx_at(2), group_id),
@@ -158,7 +161,7 @@
     def kv_wait(r, part):
         kv_copy(r, part, own_kv).wait_recv()
 
-    for part in range(2):
+    for part in range(4):
 
         @pl.when(room_for(2))
         def _():
@@ -201,6 +204,24 @@
     for r in OFFSETS:
         mask_rows(r)
 
+    def pass_on(part):
+        kv_wait(1, part)
+
+        @pl.when(room_for(2))
+        def _():
+            kv_copy(3, part, got_kv.at[0]).start()
+
+    @pl.when(parity == 1)
+    def _():
+        for part in range(4):
+
+            @pl.when(at_least(2))
+            def _():
+                kv_wait(2, part)
+                kv_copy(1, part, got_kv.at[1]).start()
+
+            pass_on(part)
+
     for copy in head_loads:
         copy.wait()
     norm_load.wait()
@@ -214,26 +235,6 @@
             push = jnp.where(active, jnp.float32(0.0), jnp.float32(1e30))
             rows_buf[r + 1 : r + 2, rows] = norm_in[h : h + 1, :] + push
 
-    @pl.when((parity == 1) & at_least(2))
-    def _():
-        for part in range(2):
-            kv_wait(2, part)
-            kv_copy(1, part, got_kv.at[1]).start()
-
-    @pl.when(at_least(1))
-    def _():
-        for part in range(2):
-            kv_wait(1, part)
-
-            @pl.when(room_for(2))
-            def _():
-                kv_copy(3, part, got_kv.at[0]).start()
-
-    @pl.when((parity == 0) & at_least(2))
-    def _():
-        for part in range(2):
-            kv_wait(2, part)
-
     def back_copy(r, half):
         return pltpu.make_async_remote_copy(
             src_ref=back_out.at[r - 1, half],
@@ -245,16 +246,19 @@
         )
 
     def pair_grads(r):
-        if r == 3:
-            for part in range(2):
-                kv_wait(3, part)
         if r > 0:
             key_blk = got_kv.at[r - 1, 0]
             value_blk = got_kv.at[r - 1, 1]
         else:
             key_blk = own_kv.at[0]
             value_blk = own_kv.at[1]
+        if r == 3:
+            for part in range(2):
+                kv_wait(3, part)
         s_buf[...] = dot(key_blk[...], q_st[...], NT)
+        if r == 3:
+            for part in range(2, 4):
+                kv_wait(3, part)
         dp_buf[...] = dot(value_blk[...], g_st[...], NT)
 
         def pair_rows(i, carry, r=r):
@@ -287,7 +291,24 @@
         dq_acc[...] += add_query
 
     dq_acc[...] = jnp.zeros_like(dq_acc)
+    @pl.when(block_id == 2)
+    def _():
+        for part in range(4):
+            pass_on(part)
+
+    @pl.when((parity == 0) & at_least(2))
+    def _():
+        for part in range(4):
+            kv_wait(2, part)
+
     for r in OFFSETS:
+        if r == 1:
+
+            @pl.when((parity == 0) & at_least(4))
+            def _():
+                for part in range(4):
+                    pass_on(part)
+
         if r == 0:
             pair_grads(r)
         else:
@@ -417,9 +438,9 @@
         lax.fori_loop(0, half_rows // ROWS, last_rows, 0)
 
     sends = (
-        (room_for(2), [kv_copy(2, part, own_kv) for part in range(2)]),
-        ((parity == 0) | at_least(2), [kv_copy(1, part, own_kv) for part in range(2)]),
-        (at_least(1) & room_for(2), [kv_copy(3, part, own_kv) for part in range(2)]),
+        (room_for(2), [kv_copy(2, part, own_kv) for part in range(4)]),
+        ((parity == 0) | at_least(2), [kv_copy(1, part, own_kv) for part in range(4)]),
+        (at_least(1) & room_for(2), [kv_copy(3, part, own_kv) for part in range(4)]),
     )
     sends += tuple((at_least(r), [back_copy(r, half) for half in range(2)]) for r in (1, 2, 3))
     for sent, copies in sends:
@@ -482,8 +503,8 @@
             pltpu.VMEM((2, 7, tok // 2, width // 16), bf16),
             pltpu.VMEM((2, 7, tok // 2, width // 16), bf16),
             dma((2 + 3 * heads + 1 + 3,)),
-            dma((3, 2)),
-            dma((3, 2)),
+            dma((3, 4)),
+            dma((3, 4)),
             dma((3, 2)),
             dma((3, 2)),
             dma((2, 8)),

time: 45.1 us -> 44.9 us (level)
  the two profiles are of different devices: /device:TPU:450 before, /device:TPU:32 now
where the time goes in v5:
time: 44.9 us; the launch traced here: 44.7 us
  Pallas kernels  44 us (98%)
  other arithmetic  0.67 us (1%)
    pallas_call x1, Pallas kernels, on_device(): pl.pallas_call(kernel, out_shape=jax.ShapeDtypeStruct((tok, width // 16),...  44 us

profile of v5, /device:TPU:32, one launch (start us, length us, event | category | flops | bytes accessed | tf_op | source)
XLA Modules:
  0.0 44.7 jit_solution(5872037292849885720)
XLA Ops:
  0.0 44.0 %shard_map.109 = f32[256,256]{1,0:T(8,128)S(1)} custom-call(bf16[256,512]{1,0:T(8,128)(2,1)} %q_hbm.1, bf16[256,128]{1,0:T(8,128)(2,1)} %k_hbm.1, bf16[256,128]{1,0:T(8,128)(2,1)} %v_hbm.1, bf16[256,512]{1,0:T(8,128)(2,1)} %o_hbm.1, bf16[256,512]{1,0:T(8,128)(2,1)} %g_hbm.1, f32[4,256]{1,0:T(4,128)} %bitcast.1, s32[1,4]{1,0:T(1,128)} %mask_smem.1, ...), custom_call_target="tpu_custom_call" | custom-call | tf_op jit(solution)/shard_map/pallas_call | solution.py:473
  44.0 0.7 %convert_element_type.3 = bf16[256,256]{1,0:T(8,128)(2,1)} convert(f32[256,256]{1,0:T(8,128)S(1)} %shard_map.109) | non-fusion elementwise | flops 65536 | bytes 393216 | tf_op jit(solution)/shard_map/convert_element_type | solution.py:521

commit v6 on v5

--- a/solution.py
+++ b/solution.py
@@ -15,7 +15,7 @@
 NN = (((1,), (0,)), ((), ()))
 TN = (((0,), (0,)), ((), ()))
 HOPS = ((2, 1), (1, 1), (3, 1), (0, 1), (2, 0), (1, 0), (3, 0), (0, 0))
-OFFSETS = (2, 1, 0, 3)
+ORDER = ((2, 3, None), (1, 2, None), (0, 0, None), (3, 3, None), (2, 2, 2), (1, 1, 1))
 
 
 def dot(a, b, dims):
@@ -29,8 +29,8 @@
     o_hbm,
     g_hbm,
     norm_hbm,
-    mask_smem,
-    base_smem,
+    mask_hbm,
+    base_hbm,
     wq_hbm,
     wk_hbm,
     wv_hbm,
@@ -39,6 +39,8 @@
     g_st,
     o_st,
     norm_in,
+    mask_smem,
+    base_smem,
     own_kv,
     got_kv,
     kept,
@@ -109,6 +111,7 @@
         loads.append(copy)
         return copy
 
+    small_loads = [load(mask_hbm, mask_smem), load(base_hbm, base_smem)]
     kv_loads = [load(k_hbm, own_kv.at[0]), load(v_hbm, own_kv.at[1])]
     head_loads = []
     for src, dst in ((g_hbm, g_st), (o_hbm, o_st), (q_hbm, q_st)):
@@ -171,6 +174,9 @@
         def _():
             kv_copy(1, part, own_kv).start()
 
+    for copy in small_loads:
+        copy.wait()
+
     lane = lax.broadcasted_iota(jnp.int32, (ROWS, wide), 1)
     sub = lax.broadcasted_iota(jnp.int32, (ROWS, wide), 0)
     head = lane // tok
@@ -201,7 +207,7 @@
 
         lax.fori_loop(0, tok // ROWS, step, 0)
 
-    for r in OFFSETS:
+    for r in (2, 1, 0, 3):
         mask_rows(r)
 
     def pass_on(part):
@@ -296,25 +302,34 @@
         for part in range(4):
             pass_on(part)
 
-    @pl.when((parity == 0) & at_least(2))
+    @pl.when((parity == 0) & at_least(3))
     def _():
         for part in range(4):
             kv_wait(2, part)
 
-    for r in OFFSETS:
-        if r == 1:
-
-            @pl.when((parity == 0) & at_least(4))
+    for r, first, last in ORDER:
+        if r == 1 and last is None:
+
+            @pl.when((parity == 0) & at_least(3))
             def _():
                 for part in range(4):
                     pass_on(part)
 
         if r == 0:
             pair_grads(r)
+        elif last is None:
+
+            @pl.when(at_least(first))
+            def _():
+                pair_grads(r)
+
         else:
 
-            @pl.when(at_least(r))
+            @pl.when(block_id == first)
             def _():
+                if r == 2:
+                    for part in range(4):
+                        kv_wait(2, part)
                 pair_grads(r)
 
     for h in range(heads):
@@ -353,9 +368,12 @@
         copy.start()
         pair_copies[j, half] = copy
 
+    def y_first(half):
+        return core if half == 0 else 1 - core
+
     def far_copy(j, half):
         if j < 3:
-            hop_y, hop_x = core * HOPS[j][0], 1 - core
+            hop_y, hop_x = y_first(half) * HOPS[j][0], 1 - y_first(half)
         else:
             hop_y, hop_x = HOPS[j][0], HOPS[j][1]
         return pltpu.make_async_remote_copy(
@@ -381,11 +399,9 @@
                 own_acc[at, :] += back_in[r - 1, half].astype(jnp.float32)
 
         kv_grads[at, :] = own_acc[at, :].astype(jnp.bfloat16)
-        send_pair(0, half)
-        send_pair(1, half)
         for j in range(8):
-            if j + 2 < 8:
-                send_pair(j + 2, half)
+            send_pair(j, half)
+        for j in range(8):
             own = term(chip_at(HOPS[j]) * 2 + core, half)
             pair_copies[j, half].wait_recv()
             own = own + pair_in[half, j].astype(jnp.float32)
@@ -395,21 +411,21 @@
                 sums[j - 3, at, :] = own
             if 3 <= j < 7:
 
-                @pl.when(core == (0 if j == 3 else 1))
+                @pl.when(y_first(half) == (0 if j == 3 else 1))
                 def _():
                     send_far(j, half, sums[j - 3, at, :])
 
     def second_phase(half):
         at = halves[half]
 
-        @pl.when(core == 0)
+        @pl.when(y_first(half) == 0)
         def _():
             for j in range(3):
                 far_copy(j, half).wait_recv()
                 value = sums[j + 1, at, :] + far_in[half, j].astype(jnp.float32)
                 send_far(j + 4, half, value)
 
-        @pl.when(core == 1)
+        @pl.when(y_first(half) == 1)
         def _():
             total = sums[0, at, :]
             for j in range(3):
@@ -465,7 +481,6 @@
     wide = heads * tok
     width = q_weight.shape[0]
     any_spec = pl.BlockSpec(memory_space=pl.ANY)
-    smem_spec = pl.BlockSpec(memory_space=pltpu.SMEM)
     bf16, f32 = jnp.bfloat16, jnp.float32
     dma = pltpu.SemaphoreType.DMA
     operands = (queries, keys, values, outputs, out_grad, log_norm.T, *args[6:])
@@ -473,13 +488,15 @@
     total = pl.pallas_call(
         kernel,
         out_shape=jax.ShapeDtypeStruct((tok, width // 16), f32),
-        in_specs=[any_spec] * 6 + [smem_spec] * 2 + [any_spec] * 3,
+        in_specs=[any_spec] * 11,
         out_specs=pl.BlockSpec(memory_space=pltpu.VMEM),
         scratch_shapes=[
             pltpu.VMEM((wide, hd), bf16),
             pltpu.VMEM((wide, hd), bf16),
             pltpu.VMEM((wide, hd), bf16),
             pltpu.VMEM((heads, tok), f32),
+            pltpu.SMEM((1, 4), jnp.int32),
+            pltpu.SMEM((2,), jnp.int32),
             pltpu.VMEM((2, tok, hd), bf16),
             pltpu.VMEM((3, 2, tok, hd), bf16),
             pltpu.VMEM((4, tok, wide), f32),
@@ -502,7 +519,7 @@
             pltpu.VMEM((2, 8, tok // 2, width // 16), bf16),
             pltpu.VMEM((2, 7, tok // 2, width // 16), bf16),
             pltpu.VMEM((2, 7, tok // 2, width // 16), bf16),
-            dma((2 + 3 * heads + 1 + 3,)),
+            dma((2 + 2 + 3 * heads + 1 + 3,)),
             dma((3, 4)),
             dma((3, 4)),
             dma((3, 2)),

time: 44.9 us -> 46.2 us (1.029)
  the two profiles are of different devices: /device:TPU:32 before, /device:TPU:8 now
where the time goes in v6:
time: 46.2 us; the launch traced here: 46.1 us
  Pallas kernels  45.4 us (98%)
  other arithmetic  0.67 us (1%)
    pallas_call x1, Pallas kernels, on_device(): pl.pallas_call(kernel, out_shape=jax.ShapeDtypeStruct((tok, width // 16),...  45.4 us

profile of v6, /device:TPU:8, one launch (start us, length us, event | category | flops | bytes accessed | tf_op | source)
XLA Modules:
  0.0 46.1 jit_solution(14474110041882090859)
XLA Ops:
  0.0 45.4 %shard_map.109 = f32[256,256]{1,0:T(8,128)S(1)} custom-call(bf16[256,512]{1,0:T(8,128)(2,1)} %q_hbm.1, bf16[256,128]{1,0:T(8,128)(2,1)} %k_hbm.1, bf16[256,128]{1,0:T(8,128)(2,1)} %v_hbm.1, bf16[256,512]{1,0:T(8,128)(2,1)} %o_hbm.1, bf16[256,512]{1,0:T(8,128)(2,1)} %g_hbm.1, f32[4,256]{1,0:T(4,128)} %bitcast.1, s32[1,4]{1,0:T(1,128)} %mask_hbm.1, ...), custom_call_target="tpu_custom_call" | custom-call | tf_op jit(solution)/shard_map/pallas_call | solution.py:488
  45.4 0.7 %convert_element_type.3 = bf16[256,256]{1,0:T(8,128)(2,1)} convert(f32[256,256]{1,0:T(8,128)S(1)} %shard_map.109) | non-fusion elementwise | flops 65536 | bytes 393216 | tf_op jit(solution)/shard_map/convert_element_type | solution.py:538
